TPU v7x, 32 devices: a whole 2x2x4 slice. The times are simulated.
32 devices in a mesh: row: 4 (over x, core), col: 2 (over y), store: 4 (over z).
Axes of the slice: x: 2, y: 2, z: 4, core: 2. Of those that a mesh axis runs over, the one named last changes fastest.
Arguments:
- hidden: bfloat16 [128, 128, 4096], P('store', 'row', 'col'), may hold values from -6 to 6
- out_grads: bfloat16 [208, 128, 128], P('row', 'store'), may hold values from -6 to 6
- proj_out: bfloat16 [208, 64], P('row'), may hold values from -0.4375 to 0.4375
- proj_in: bfloat16 [4096, 64], P('col'), may hold values from -0.09375 to 0.09375
- lengths: int32 [128], P('store'), may hold values from 64 to 128
- precond: bfloat16 [4096, 4096], P(('row', 'col'), 'store'), may hold values from -1 to 2, as said below
- stored: bfloat16 [12288, 4096], P(('row', 'col', 'store')), may hold values from -0.09375 to 0.09375
Outputs:
- scores: float32 [128, 12288], P(None, ('row', 'col', 'store'))
Inputs may be any that keep to these rules, and one draw needn't show every extreme that they name: Query q's live tokens are its first lengths[q] token slots. precond is symmetric.
All inputs are finite; a program needn't handle non-finite values.
Results may differ from a plain program's by a relative error of at most 0.0057.
Values may be sent and summed in bfloat16 or wider, within the bound.
No kernel may reach another device: no remote copies, remote signals or barrier semaphores. Data moves between devices by JAX's collectives and lax.ppermute only.
A program may use at most 64 MiB of HBM per device.

v0:
```python
import jax
import jax.numpy as jnp
from jax import lax
from jax.sharding import PartitionSpec as P

TOK = 128


def on_device(hidden, out_grads, proj_out, proj_in, lengths, precond, stored):
    queries, token_part, columns = hidden.shape
    width_in = proj_in.shape[1]
    local_proj = jnp.einsum(
        "qtc,cb->qtb", hidden, proj_in, preferred_element_type=jnp.float32
    ).astype(jnp.bfloat16)
    flattened = local_proj.reshape(queries, token_part * width_in)
    inputs_all = lax.all_gather(flattened, "row", axis=1, tiled=True).reshape(queries, -1, width_in)
    tokens = inputs_all.shape[1]
    position = jnp.arange(tokens, dtype=jnp.int32)
    live_mask = (position[None, :] < lengths[:, None]).astype(jnp.float32)
    outputs_proj = jnp.einsum(
        "rqt,ra->qta", out_grads, proj_out, preferred_element_type=jnp.float32
    )
    outputs_proj = (outputs_proj * live_mask[:, :, None]).astype(jnp.bfloat16)
    partial_value = jnp.einsum(
        "qta,qtb->qab", outputs_proj, inputs_all, preferred_element_type=jnp.float32
    )
    partial_value = partial_value.reshape(queries, -1) * TOK ** (-0.5)
    shares = lax.psum_scatter(
        partial_value, ("row", "col"), scatter_dimension=1, tiled=True
    ).astype(jnp.bfloat16)
    cond_terms = jnp.dot(
        shares,
        lax.all_gather(precond, "store", axis=1, tiled=True),
        preferred_element_type=jnp.float32,
    )
    conditioned = lax.psum_scatter(
        cond_terms, ("row", "col"), scatter_dimension=1, tiled=True
    ).astype(jnp.bfloat16)
    full_features = lax.all_gather(conditioned, ("row", "col"), axis=1, tiled=True)
    return lax.dot_general(
        lax.all_gather(full_features, "store", axis=0, tiled=True),
        stored,
        (((1,), (1,)), ((), ())),
        preferred_element_type=jnp.float32,
    )


def solution(mesh):
    return jax.shard_map(
        on_device,
        mesh=mesh,
        in_specs=(
            P("store", "row", "col"),
            P("row", "store", None),
            P("row", None),
            P("col", None),
            P("store"),
            P(("row", "col"), "store"),
            P(("row", "col", "store"), None),
        ),
        out_specs=P(None, ("row", "col", "store")),
        check_vma=False,
    )
```

profile of v0, /device:TPU:0, one launch (start us, length us, event | category | flops | bytes accessed | tf_op | source)
XLA Modules:
  0.0 207.3 jit_solution(10469774446894021144)
XLA Ops:
  7.4 0.0 copy-start
  7.4 0.0 copy-start.1
  7.4 0.0 reduce-scatter.3.cloned.1.call-start
  7.4 3.6 %convolution_convert_fusion = bf16[32,32,64]{2,1,0:T(8,128)(2,1)S(1)} fusion(bf16[32,32,2048]{2,1,0:T(8,128)(2,1)} %param.7, bf16[2048,64]{0,1:T(8,128)(2,1)} %param.10), kind=kOutput, calls=%fused_computation.3 | convolution fusion | flops 268500992 | bytes 4587520 | tf_op jit(solution)/shard_map/qtc,cb->qtb/dot_general | solution.py:12
  11.0 0.3 reshape.31
  11.3 9.1 %all_gather.12 = bf16[32,8192]{1,0:T(8,128)(2,1)} all-gather(bf16[32,2048]{1,0:T(8,128)(2,1)S(1)} %reshape.31), channel_id=1, replica_groups=mesh['row'=4,'col'=2,'store'=4] {'row'}, dimensions={1}, use_global_device_ids=true | all-gather | bytes 655360 | tf_op jit(solution)/shard_map/all_gather | solution.py:16
  20.3 2.7 %reshape.32 = bf16[32,128,64]{2,1,0:T(8,128)(2,1)} reshape(bf16[32,8192]{1,0:T(8,128)(2,1)} %all_gather.12) | data formatting | bytes 1048576 | tf_op jit(solution)/shard_map/reshape | solution.py:16
  23.1 0.7 fusion.7
  23.8 0.0 copy-done.1
  23.8 3.0 %convolution_multiply_fusion.1 = f32[32,64,64]{2,1,0:T(8,128)} fusion(bf16[32,128,64]{2,1,0:T(8,128)(2,1)} %reshape.32, f32[32,128]{1,0:T(8,128)S(1)} %fusion.7, bf16[52,32,128]{2,1,0:T(8,128)(2,1)} %param.8, bf16[52,64]{1,0:T(8,128)(2,1)S(1)} %copy-done.1), kind=kOutput, calls=%fused_computation.1 | convolution fusion | flops 61472768 | bytes 1497600 | tf_op jit(solution)/shard_map/qta,qtb->qab/dot_general | solution.py:24
  26.8 2.4 %mul.21 = f32[32,4096]{1,0:T(8,128)} reshape(f32[32,64,64]{2,1,0:T(8,128)} %convolution_multiply_fusion.1) | data formatting | bytes 1048576 | tf_op jit(solution)/shard_map/mul | solution.py:27
  29.2 0.0 reduce-scatter.3.cloned.1.call-update
  29.3 0.0 all-gather.3.cloned.1.call-start
  29.3 0.5 all-gather.3.cloned.1.call-update
  29.8 0.0 reduce-scatter.5.cloned.1.call-start
  29.9 34.5 %reduce-scatter.3.cloned.1.call-done = f32[32,512]{1,0:T(8,128)} async-done(((f32[32,4096]{1,0:T(8,128)}), f32[32,512]{1,0:T(8,128)}) %reduce-scatter.3.cloned.1.call-update) | async-done | bytes 65552 | tf_op jit(solution)/shard_map/reduce_scatter | solution.py:28
  64.4 48.4 %all-gather.3.cloned.1.call-done = bf16[512,4096]{1,0:T(8,128)(2,1)} async-done(((bf16[512,1024]{1,0:T(8,128)(2,1)}), bf16[512,4096]{1,0:T(8,128)(2,1)}) %all-gather.3.cloned.1.call-update) | async-done | bytes 4194320 | tf_op jit(solution)/shard_map/all_gather | solution.py:33
  112.8 3.9 %fusion.5 = f32[32,4096]{1,0:T(8,128)} fusion(bf16[512,4096]{1,0:T(8,128)(2,1)} %all-gather.3.cloned.1.call-done, f32[32,512]{1,0:T(8,128)} %reduce-scatter.3.cloned.1.call-done), kind=kOutput, calls=%fused_computation.7 | convolution fusion | flops 134234112 | bytes 4784128 | tf_op jit(solution)/shard_map/dot_general | solution.py:31
  116.7 0.0 reduce-scatter.5.cloned.1.call-update
  116.7 0.0 all-gather.5.cloned.1.call-start
  116.7 32.7 %reduce-scatter.5.cloned.1.call-done = f32[32,512]{1,0:T(8,128)} async-done(((f32[32,4096]{1,0:T(8,128)}), f32[32,512]{1,0:T(8,128)}) %reduce-scatter.5.cloned.1.call-update) | async-done | bytes 65552 | tf_op jit(solution)/shard_map/reduce_scatter | solution.py:36
  149.4 0.8 convert_element_type.23
  150.3 18.6 %all_gather.14 = bf16[32,4096]{1,0:T(8,128)(2,1)} all-gather(bf16[32,512]{1,0:T(8,128)(2,1)S(1)} %convert_element_type.23), channel_id=1, replica_groups=mesh['row'=4,'col'=2,'store'=4] {'row','col'}, dimensions={1}, use_global_device_ids=true | all-gather | bytes 294912 | tf_op jit(solution)/shard_map/all_gather | solution.py:39
  168.9 0.0 all-gather.5.cloned.1.call-update
  168.9 28.0 %all-gather.5.cloned.1.call-done = bf16[128,4096]{1,0:T(8,128)(2,1)} async-done(((bf16[32,4096]{1,0:T(8,128)(2,1)}), bf16[128,4096]{1,0:T(8,128)(2,1)}) %all-gather.5.cloned.1.call-update) | async-done | bytes 1048592 | tf_op jit(solution)/shard_map/all_gather | solution.py:41
  196.9 0.0 copy-done
  196.9 3.0 %fusion.10 = f32[128,384]{1,0:T(8,128)} fusion(bf16[128,4096]{1,0:T(8,128)(2,1)} %all-gather.5.cloned.1.call-done, bf16[384,4096]{1,0:T(8,128)(2,1)S(1)} %copy-done), kind=kOutput, calls=%fused_computation.12 | convolution fusion | flops 402653184 | bytes 4390912 | tf_op jit(solution)/shard_map/dot_general | solution.py:40
Async XLA Ops:
  7.4 189.6 %copy-start = (bf16[384,4096]{1,0:T(8,128)(2,1)S(1)}, bf16[384,4096]{1,0:T(8,128)(2,1)}, u32[]{:S(2)}) copy-start(bf16[384,4096]{1,0:T(8,128)(2,1)} %param.13) | copy-start | bytes 9437188
  7.4 16.5 %copy-start.1 = (bf16[52,64]{1,0:T(8,128)(2,1)S(1)}, bf16[52,64]{1,0:T(8,128)(2,1)}, u32[]{:S(2)}) copy-start(bf16[52,64]{1,0:T(8,128)(2,1)} %param.9) | copy-start | bytes 19972
  7.4 57.0 %reduce-scatter.3.cloned.1.call-start = ((), (), s32[]{:S(2)}) async-start(), calls=%async_computation.2 | async-start | bytes 589824 | tf_op jit(solution)/shard_map/reduce_scatter | solution.py:28
  29.3 83.5 %all-gather.3.cloned.1.call-start = ((), (), s32[]{:S(2)}) async-start(), calls=%async_computation.3 | async-start | bytes 5242880 | tf_op jit(solution)/shard_map/all_gather | solution.py:33
  29.8 119.6 %reduce-scatter.5.cloned.1.call-start = ((), (), s32[]{:S(2)}) async-start(), calls=%async_computation.4 | async-start | bytes 589824 | tf_op jit(solution)/shard_map/reduce_scatter | solution.py:36
  116.7 80.2 %all-gather.5.cloned.1.call-start = ((), (), s32[]{:S(2)}) async-start(), calls=%async_computation.5 | async-start | bytes 1310720 | tf_op jit(solution)/shard_map/all_gather | solution.py:41
Sparse Core Ops, SparseCore 0:
  29.4 34.9 reduce-scatter.2
  116.8 32.5 reduce-scatter.4
Sparse Core Ops, SparseCore 1:
  31.3 81.4 all-gather.2
  169.0 27.9 all-gather.4
where the time goes:
time: 208 us; the launch traced here: 207 us
  waiting for transfers between devices  144 us (69%)
  blocking collectives  27.7 us (13%)
  between operations  14.9 us (7%)
  matrix products  13.4 us (6%)
  local copies, waits for them, and re-layouts  5.42 us (3%)
    all_gather x1, waiting for transfers between devices, on_device(): lax.all_gather(precond, 'store', axis=1, tiled=True)  48.4 us
    reduce_scatter x1, waiting for transfers between devices, on_device(): lax.psum_scatter(partial_value, ('row', 'col'), scatter_dimension=1, tile...  34.5 us
    reduce_scatter x1, waiting for transfers between devices, on_device(): lax.psum_scatter(cond_terms, ('row', 'col'), scatter_dimension=1, tiled=T...  32.7 us
    all_gather x1, waiting for transfers between devices, on_device(): lax.all_gather(full_features, 'store', axis=0, tiled=True)  28 us
    all_gather x1, blocking collectives, on_device(): lax.all_gather(conditioned, ('row', 'col'), axis=1, tiled=True)  18.6 us
    all_gather x1, blocking collectives, on_device(): lax.all_gather(flattened, 'row', axis=1, tiled=True)  9.09 us
  transfers between devices with their start and end apart: 4, of which 4 were waited for; matrix products, arithmetic and copies ran while one was open for 0% of the time, Pallas kernels for 0%

commit v1 on v0

--- a/solution.py
+++ b/solution.py
@@ -30,7 +30,7 @@
     ).astype(jnp.bfloat16)
     cond_terms = jnp.dot(
         shares,
-        lax.all_gather(precond, "store", axis=1, tiled=True),
+        jnp.concatenate(lax.all_gather(precond, "store"), axis=1),
         preferred_element_type=jnp.float32,
     )
     conditioned = lax.psum_scatter(

time: 208 us -> 195 us (0.938)
  waiting for transfers between devices: 144 us -> 125 us
  local copies, waits for them, and re-layouts: 5.42 us -> 11.7 us
    reduce_scatter x1, waiting for transfers between devices: 34.5 us -> 0.01 us  [on_device(): lax.psum_scatter(partial_value, ('row', 'col'), scatter_dimension=1, tile...]
    all_gather x1, waiting for transfers between devices: 48.4 us -> 63.2 us  [on_device(): lax.all_gather(precond, 'store')]
    reshape x0 -> x1, local copies, waits for them, and re-layouts: none -> 6.25 us  [on_device(): jnp.concatenate(lax.all_gather(precond, 'store'), axis=1)]
  transfers between devices with their start and end apart: 4 -> 4, of which waited for: 4 -> 3; matrix products, arithmetic and copies ran while one was open for 0% -> 10% of each run, Pallas kernels for 0% -> 0%
where the time goes in v1:
time: 195 us
  waiting for transfers between devices  125 us (64%)
  blocking collectives  27.7 us (14%)
  between operations  14.9 us (8%)
  matrix products  13.9 us (7%)
  local copies, waits for them, and re-layouts  11.7 us (6%)
    all_gather x1, waiting for transfers between devices, on_device(): lax.all_gather(precond, 'store')  63.2 us
    reduce_scatter x1, waiting for transfers between devices, on_device(): lax.psum_scatter(cond_terms, ('row', 'col'), scatter_dimension=1, tiled=T...  32.6 us
    all_gather x1, waiting for transfers between devices, on_device(): lax.all_gather(full_features, 'store', axis=0, tiled=True)  28.2 us
    all_gather x1, blocking collectives, on_device(): lax.all_gather(conditioned, ('row', 'col'), axis=1, tiled=True)  18.6 us
    all_gather x1, blocking collectives, on_device(): lax.all_gather(flattened, 'row', axis=1, tiled=True)  9.09 us
    reshape x1, local copies, waits for them, and re-layouts, on_device(): jnp.concatenate(lax.all_gather(precond, 'store'), axis=1)  6.25 us
    dot_general x1, matrix products, on_device(): jnp.dot(shares, jnp.concatenate(lax.all_gather(precond, 'store'), axis=1)...  4.36 us
  transfers between devices with their start and end apart: 4, of which 3 were waited for; matrix products, arithmetic and copies ran while one was open for 10% of the time, Pallas kernels for 0%

profile of v1, /device:TPU:0, one launch (start us, length us, event | category | flops | bytes accessed | tf_op | source)
XLA Modules:
  0.0 194.6 jit_solution(18022620711826235463)
XLA Ops:
  7.4 0.0 copy-start
  7.4 0.0 copy-start.1
  7.4 0.0 all-gather.6.cloned.1.call-start
  7.4 0.7 all-gather.6.cloned.1.call-update
  8.1 0.0 reduce-scatter.3.cloned.1.call-start
  8.1 3.6 %convolution_convert_fusion = bf16[32,32,64]{2,1,0:T(8,128)(2,1)S(1)} fusion(bf16[32,32,2048]{2,1,0:T(8,128)(2,1)} %param.7, bf16[2048,64]{0,1:T(8,128)(2,1)} %param.10), kind=kOutput, calls=%fused_computation.3 | convolution fusion | flops 268500992 | bytes 4587520 | tf_op jit(solution)/shard_map/qtc,cb->qtb/dot_general | solution.py:12
  11.7 0.3 reshape.37
  12.0 9.1 %all_gather.15 = bf16[32,8192]{1,0:T(8,128)(2,1)} all-gather(bf16[32,2048]{1,0:T(8,128)(2,1)S(1)} %reshape.37), channel_id=1, replica_groups=mesh['row'=4,'col'=2,'store'=4] {'row'}, dimensions={1}, use_global_device_ids=true | all-gather | bytes 655360 | tf_op jit(solution)/shard_map/all_gather | solution.py:16
  21.1 2.7 %reshape.38 = bf16[32,128,64]{2,1,0:T(8,128)(2,1)} reshape(bf16[32,8192]{1,0:T(8,128)(2,1)} %all_gather.15) | data formatting | bytes 1048576 | tf_op jit(solution)/shard_map/reshape | solution.py:16
  23.9 0.7 fusion.7
  24.6 0.0 copy-done.1
  24.6 3.0 %convolution_multiply_fusion.1 = f32[32,64,64]{2,1,0:T(8,128)} fusion(bf16[32,128,64]{2,1,0:T(8,128)(2,1)} %reshape.38, f32[32,128]{1,0:T(8,128)S(1)} %fusion.7, bf16[52,32,128]{2,1,0:T(8,128)(2,1)} %param.8, bf16[52,64]{1,0:T(8,128)(2,1)S(1)} %copy-done.1), kind=kOutput, calls=%fused_computation.1 | convolution fusion | flops 61472768 | bytes 1497600 | tf_op jit(solution)/shard_map/qta,qtb->qab/dot_general | solution.py:24
  27.6 2.4 %mul.21 = f32[32,4096]{1,0:T(8,128)} reshape(f32[32,64,64]{2,1,0:T(8,128)} %convolution_multiply_fusion.1) | data formatting | bytes 1048576 | tf_op jit(solution)/shard_map/mul | solution.py:27
  30.0 0.0 reduce-scatter.3.cloned.1.call-update
  30.0 0.0 reduce-scatter.5.cloned.1.call-start
  30.1 63.2 %all-gather.6.cloned.1.call-done = bf16[2048,1024]{1,0:T(8,128)(2,1)} async-done(((bf16[512,1024]{1,0:T(8,128)(2,1)}), bf16[2048,1024]{1,0:T(8,128)(2,1)}) %all-gather.6.cloned.1.call-update) | async-done | bytes 4194320 | tf_op jit(solution)/shard_map/all_gather | solution.py:33
  93.2 6.3 %copy.11 = bf16[512,4,1024]{0,2,1:T(8,128)(2,1)} copy(bf16[512,4,1024]{2,0,1:T(8,128)(2,1)} %bitcast.17) | data formatting | bytes 8388608 | tf_op jit(solution)/shard_map/reshape | solution.py:33
  99.5 0.0 reduce-scatter.3.cloned.1.call-done
  99.5 4.4 %fusion.5 = f32[32,4096]{1,0:T(8,128)} fusion(bf16[512,4096]{0,1:T(8,128)(2,1)} %bitcast.16, f32[32,512]{1,0:T(8,128)} %reduce-scatter.3.cloned.1.call-done), kind=kOutput, calls=%fused_computation.7 | convolution fusion | flops 134234112 | bytes 4784128 | tf_op jit(solution)/shard_map/dot_general | solution.py:31
  103.8 0.0 reduce-scatter.5.cloned.1.call-update
  103.9 0.0 all-gather.4.cloned.1.call-start
  103.9 32.6 %reduce-scatter.5.cloned.1.call-done = f32[32,512]{1,0:T(8,128)} async-done(((f32[32,4096]{1,0:T(8,128)}), f32[32,512]{1,0:T(8,128)}) %reduce-scatter.5.cloned.1.call-update) | async-done | bytes 65552 | tf_op jit(solution)/shard_map/reduce_scatter | solution.py:36
  136.6 0.8 convert_element_type.23
  137.4 18.6 %all_gather.18 = bf16[32,4096]{1,0:T(8,128)(2,1)} all-gather(bf16[32,512]{1,0:T(8,128)(2,1)S(1)} %convert_element_type.23), channel_id=1, replica_groups=mesh['row'=4,'col'=2,'store'=4] {'row','col'}, dimensions={1}, use_global_device_ids=true | all-gather | bytes 294912 | tf_op jit(solution)/shard_map/all_gather | solution.py:39
  156.0 0.0 all-gather.4.cloned.1.call-update
  156.0 28.2 %all-gather.4.cloned.1.call-done = bf16[128,4096]{1,0:T(8,128)(2,1)} async-done(((bf16[32,4096]{1,0:T(8,128)(2,1)}), bf16[128,4096]{1,0:T(8,128)(2,1)}) %all-gather.4.cloned.1.call-update) | async-done | bytes 1048592 | tf_op jit(solution)/shard_map/all_gather | solution.py:41
  184.2 0.0 copy-done
  184.2 3.0 %fusion.10 = f32[128,384]{1,0:T(8,128)} fusion(bf16[128,4096]{1,0:T(8,128)(2,1)} %all-gather.4.cloned.1.call-done, bf16[384,4096]{1,0:T(8,128)(2,1)S(1)} %copy-done), kind=kOutput, calls=%fused_computation.12 | convolution fusion | flops 402653184 | bytes 4390912 | tf_op jit(solution)/shard_map/dot_general | solution.py:40
Async XLA Ops:
  7.4 176.8 %copy-start = (bf16[384,4096]{1,0:T(8,128)(2,1)S(1)}, bf16[384,4096]{1,0:T(8,128)(2,1)}, u32[]{:S(2)}) copy-start(bf16[384,4096]{1,0:T(8,128)(2,1)} %param.13) | copy-start | bytes 9437188
  7.4 17.2 %copy-start.1 = (bf16[52,64]{1,0:T(8,128)(2,1)S(1)}, bf16[52,64]{1,0:T(8,128)(2,1)}, u32[]{:S(2)}) copy-start(bf16[52,64]{1,0:T(8,128)(2,1)} %param.9) | copy-start | bytes 19972
  7.4 85.9 %all-gather.6.cloned.1.call-start = ((), (), s32[]{:S(2)}) async-start(), calls=%async_computation.5 | async-start | bytes 5242880 | tf_op jit(solution)/shard_map/all_gather | solution.py:33
  8.1 91.4 %reduce-scatter.3.cloned.1.call-start = ((), (), s32[]{:S(2)}) async-start(), calls=%async_computation.2 | async-start | bytes 589824 | tf_op jit(solution)/shard_map/reduce_scatter | solution.py:28
  30.0 106.5 %reduce-scatter.5.cloned.1.call-start = ((), (), s32[]{:S(2)}) async-start(), calls=%async_computation.3 | async-start | bytes 589824 | tf_op jit(solution)/shard_map/reduce_scatter | solution.py:36
  103.9 80.3 %all-gather.4.cloned.1.call-start = ((), (), s32[]{:S(2)}) async-start(), calls=%async_computation.4 | async-start | bytes 1310720 | tf_op jit(solution)/shard_map/all_gather | solution.py:41
Sparse Core Ops, SparseCore 0:
  9.7 83.4 all-gather.5
  156.2 27.9 all-gather.3
Sparse Core Ops, SparseCore 1:
  30.1 34.9 reduce-scatter.2
  104.0 32.5 reduce-scatter.4
